TPU v7x, 32 devices: a whole 2x2x4 slice. The times are simulated.
32 devices in a mesh: toa: 16 (over z, y, x), rep: 2 (over core).
Axes of the slice: x: 2, y: 2, z: 4, core: 2. Of those that a mesh axis runs over, the one named last changes fastest.
Arguments:
- residual: float32 [2048, 256], P('toa'), may hold values from -6 to 6
- toa_error: float32 [2048, 256], P('toa'), may hold values from 0.3 to 3
- basis_rows: bfloat16 [2048, 100, 256], P('toa', 'rep'), may hold values from -0.041432038 to 0.041432038
- efac_table: float32 [16, 64], replicated, may hold values from 0.5 to 2
- equad_table: float32 [16, 64], replicated, may hold values from 0.1 to 1
- pulsar: int32 [2048], P('toa'), may hold values from 0 to 15
- backend: int32 [2048], P('toa'), may hold values from 0 to 63
- counts: int32 [2048], P('toa'), may hold values from 64 to 256
- owner_slot: int32 [2048], P('toa'), may hold values from 0 to 2047, as said below
Outputs:
- gram_matrix: float32 [16, 100, 100], P('toa', None, 'rep')
- projection: float32 [16, 100], P('toa', 'rep')
- whitened: float32 [2048, 256], P('toa')
Inputs may be any that keep to these rules, and one draw needn't show every extreme that they name: A permutation of the 2048 slots, independent of pulsar and backend; owner_slot // 128 is the device index along toa that holds the tile's output row and owner_slot % 128 its place there; each device's tiles go exactly 8 to each device.
All inputs are finite; a program needn't handle non-finite values.
Results may differ from a plain program's by a relative error of at most 0.0032.
Values may be sent and summed in bfloat16 or wider, within the bound.
A program may use at most 64 MiB of HBM per device.

v0:
```python
import jax
import jax.numpy as jnp
from jax import lax
from jax.sharding import PartitionSpec as P


def lookup(small_table, onehot_pulsar, onehot_backend):
    table_rows = jnp.dot(onehot_pulsar, small_table, precision=lax.Precision.HIGHEST)
    return jnp.sum(table_rows * onehot_backend, axis=1)


def tile_weights(residual, toa_error, pulsar, backend, counts, efac_table, equad_table):
    onehot_pulsar = (
        pulsar[:, None] == jnp.arange(efac_table.shape[0], dtype=jnp.int32)[None, :]
    ).astype(jnp.float32)
    onehot_backend = (
        backend[:, None] == jnp.arange(efac_table.shape[1], dtype=jnp.int32)[None, :]
    ).astype(jnp.float32)
    factor = lookup(efac_table, onehot_pulsar, onehot_backend)
    floor_term = lookup(equad_table, onehot_pulsar, onehot_backend)
    valid_rows = jnp.arange(residual.shape[1], dtype=jnp.int32)[None, :] < counts[:, None]
    weight = jnp.where(
        valid_rows, 1.0 / (factor[:, None] ** 2 * toa_error**2 + floor_term[:, None] ** 2), 0.0
    )
    return (onehot_pulsar, weight)


def pulsar_terms(basis_own, weight, residual, onehot_pulsar):
    scaled = (weight[:, None, :] * basis_own).astype(jnp.bfloat16)
    weighted_res = (weight * residual).astype(jnp.bfloat16)
    tile_gram = jnp.einsum(
        "tkr,tjr->tkj",
        lax.all_gather(basis_own, "rep", axis=1, tiled=True),
        scaled,
        preferred_element_type=jnp.float32,
    )
    tile_proj = jnp.einsum(
        "tjr,tr->tj", basis_own, weighted_res, preferred_element_type=jnp.float32
    )
    tile_total, full_width, half_width = tile_gram.shape
    pulsar_total = onehot_pulsar.shape[1]
    stacked = jnp.concatenate([tile_gram, tile_proj[:, None, :]], axis=1).reshape(
        tile_total, (full_width + 1) * half_width
    )
    owned_rows = pulsar_total // lax.axis_size("toa")
    summed = lax.psum_scatter(
        jnp.dot(onehot_pulsar.T, stacked, precision=lax.Precision.HIGHEST),
        "toa",
        scatter_dimension=0,
        tiled=True,
    )
    summed = summed.reshape(owned_rows, full_width + 1, half_width)
    return (summed[:, :full_width, :], summed[:, full_width, :])


def shards(
    residual, toa_error, basis_rows, efac_table, equad_table, pulsar, backend, counts, owner_slot
):
    tile_count = residual.shape[0]
    peer_count = lax.axis_size("toa")
    per_peer = tile_count // peer_count
    owner_dev = owner_slot // tile_count
    owner_place = owner_slot % tile_count
    onehot_dest = (owner_dev[:, None] == jnp.arange(peer_count, dtype=jnp.int32)[None, :]).astype(
        jnp.int32
    )
    bucket_rank = jnp.sum((jnp.cumsum(onehot_dest, axis=0) - 1) * onehot_dest, axis=1)
    send_position = owner_dev * per_peer + bucket_rank
    send_order = (
        jnp.zeros((tile_count,), jnp.int32)
        .at[send_position]
        .set(jnp.arange(tile_count, dtype=jnp.int32))
    )
    onehot_pulsar, weight = tile_weights(
        residual, toa_error, pulsar, backend, counts, efac_table, equad_table
    )
    whitened_local = jnp.sqrt(weight) * residual
    place_float = owner_place[send_order][:, None].astype(jnp.float32)
    moved_white, moved_place = (
        lax.all_to_all(whitened_local[send_order], "toa", split_axis=0, concat_axis=0, tiled=True),
        lax.all_to_all(place_float, "toa", split_axis=0, concat_axis=0, tiled=True),
    )
    whitened = jnp.zeros_like(moved_white).at[moved_place[:, 0].astype(jnp.int32)].set(moved_white)
    gram_matrix, projection = pulsar_terms(basis_rows, weight, residual, onehot_pulsar)
    return (gram_matrix, projection, whitened)


def solution(mesh):
    in_specs = (
        P("toa", None),
        P("toa", None),
        P("toa", "rep", None),
        P(),
        P(),
        P("toa"),
        P("toa"),
        P("toa"),
        P("toa"),
    )
    out_specs = (P("toa", None, "rep"), P("toa", "rep"), P("toa", None))
    return jax.shard_map(shards, mesh=mesh, in_specs=in_specs, out_specs=out_specs, check_vma=False)
```

profile of v0, /device:TPU:0, one launch (start us, length us, event | category | flops | bytes accessed | tf_op | source)
XLA Modules:
  0.0 174.3 jit_solution(13949590964436648195)
XLA Ops:
  7.2 0.0 copy-start
  7.2 0.0 copy-start.1
  7.2 0.0 copy-start.4
  7.2 0.0 copy-start.7
  7.2 0.0 copy-start.6
  7.2 0.0 all-gather.2.cloned.1.call-start
  7.3 0.7 all-gather.2.cloned.1.call-update
  8.0 0.8 and_select_fusion
  8.8 0.1 fusion.16
  8.9 0.2 reduce_window_sum.11
  9.0 0.2 select_reduce_fusion
  9.2 1.0 scatter_custom_fusion
  10.2 0.0 copy-start.3
  10.2 1.2 gather_fusion
  11.5 0.7 convert_element_type.47
  12.2 8.3 %all-to-all-start = ((f32[16,8,1]{1,2,0:T(1,128)}), f32[16,8,1]{1,2,0:T(1,128)S(1)}, u32[]{:S(2)}, u32[]{:S(2)}) async-start(f32[16,8,1]{1,2,0:T(1,128)} %bitcast.4), calls=%async_computation | async-start | bytes 16384 | tf_op jit(solution)/shard_map/all_to_all | solution.py:81
  20.5 0.0 all-reduce.3.cloned.1.call-start
  20.6 0.0 copy-done
  20.6 0.0 copy-done.4
  20.6 0.0 copy-done.7
  20.6 0.3 fusion.10
  20.9 0.0 copy-done.6
  20.9 0.3 fusion.11
  21.2 0.0 copy-done.3
  21.2 1.2 sqrt_multiply_fusion
  22.4 1.5 gather_fusion.1
  23.9 1.2 dynamic-slice
  25.2 1.0 fusion.15
  26.1 0.0 copy-done.1
  26.2 2.7 %multiply_convert_fusion = bf16[128,50,256]{2,0,1:T(8,128)(2,1)} fusion(bf16[128,50,256]{2,0,1:T(8,128)(2,1)S(1)} %copy-done.1, f32[128,256]{1,0:T(8,128)S(1)} %get-tuple-element.10), kind=kLoop, calls=%fused_computation.6 | loop fusion | flops 4915200 | bytes 6684672 | tf_op jit(solution)/shard_map/convert_element_type | solution.py:29
  28.8 4.1 %fusion.2 = f32[128,1,50]{1,2,0:T(8,128)} fusion(bf16[128,50,256]{2,0,1:T(8,128)(2,1)S(1)} %copy-done.1, bf16[128,256,1]{1,0,2:T(8,128)(2,1)S(1)} %fusion.15), kind=kOutput, calls=%fused_computation.8 | convolution fusion | flops 3276800 | bytes 3367936 | tf_op jit(solution)/shard_map/broadcast_in_dim | solution.py:42
  33.0 9.6 %fusion.5 = f32[128,100,50]{1,2,0:T(8,128)S(1)} fusion(bf16[128,100,256]{2,0,1:T(8,128)(2,1)} %all-gather.2.cloned.1.call-done, bf16[128,50,256]{2,0,1:T(8,128)(2,1)} %multiply_convert_fusion), kind=kOutput, calls=%fused_computation.11 | convolution fusion | flops 327680000 | bytes 12390400 | tf_op jit(solution)/shard_map/tkr,tjr->tkj/dot_general | solution.py:31
  42.6 2.8 %pad_maximum_fusion = f32[128,101,50]{1,2,0:T(8,128)} fusion(f32[128,1,50]{1,2,0:T(8,128)S(1)} %copy-done.2, f32[128,100,50]{1,2,0:T(8,128)S(1)} %fusion.5), kind=kLoop, calls=%fused_computation.7 | loop fusion | flops 646400 | bytes 5171200 | tf_op jit(solution)/shard_map/concatenate | solution.py:42
  45.4 3.7 %copy.23 = f32[128,101,50]{0,2,1:T(8,128)S(1)} copy(f32[128,101,50]{1,2,0:T(8,128)} %pad_maximum_fusion) | data formatting | bytes 5171200 | tf_op jit(solution)/shard_map/concatenate | solution.py:42
  49.1 0.0 copy-start.5
  49.1 1.7 reshape.61
  50.7 3.8 %fusion.19 = f32[16,5050]{1,0:T(8,128)} fusion(f32[128,5050]{0,1:T(8,128)} %reshape.61, s32[128]{0:T(128)S(1)} %copy-done.5), kind=kOutput, calls=%fused_computation.30 | convolution fusion | flops 124112896 | bytes 2909312 | tf_op jit(solution)/shard_map/dot_general | solution.py:47
  54.5 0.0 all-reduce.3.cloned.1.call-update
  54.6 0.0 all-to-all-done
  54.6 6.9 %all-to-all-start.1 = ((f32[16,8,256]{2,1,0:T(8,128)}), f32[16,8,256]{2,1,0:T(8,128)S(1)}, u32[]{:S(2)}, u32[]{:S(2)}) async-start(f32[16,8,256]{2,1,0:T(8,128)} %bitcast.6), calls=%async_computation.1 | async-start | bytes 262144 | tf_op jit(solution)/shard_map/all_to_all | solution.py:80
  61.5 0.1 convert_element_type.49
  61.6 7.7 %all-to-all-done.1 = f32[16,8,256]{2,1,0:T(8,128)S(1)} async-done(((f32[16,8,256]{2,1,0:T(8,128)}), f32[16,8,256]{2,1,0:T(8,128)S(1)}, u32[]{:S(2)}, u32[]{:S(2)}) %all-to-all-start.1) | async-done | bytes 131104 | tf_op jit(solution)/shard_map/all_to_all | solution.py:80
  69.3 1.6 scatter_custom_fusion.1
  70.9 93.5 %all-reduce.3.cloned.1.call-done = f32[16,5050]{1,0:T(8,128)} async-done(((f32[16,5050]{1,0:T(8,128)}), f32[16,5050]{1,0:T(8,128)}) %all-reduce.3.cloned.1.call-update) | async-done | bytes 323216
  164.4 1.6 dynamic-slice_reduce_fusion
  166.1 0.1 reshape.62
  166.2 0.5 slice_bitcast_fusion
  166.7 0.7 copy.25
  (13 shorter events, 0.1 us)
Async XLA Ops:
  7.2 13.4 %copy-start = (f32[16,64]{1,0:T(8,128)S(1)}, f32[16,64]{1,0:T(8,128)}, u32[]{:S(2)}) copy-start(f32[16,64]{1,0:T(8,128)} %param.12) | copy-start | bytes 12292
  7.2 19.0 %copy-start.1 = (bf16[128,50,256]{2,0,1:T(8,128)(2,1)S(1)}, bf16[128,50,256]{2,0,1:T(8,128)(2,1)}, u32[]{:S(2)}) copy-start(bf16[128,50,256]{2,0,1:T(8,128)(2,1)} %param.11) | copy-start | bytes 9830404
  7.2 13.4 %copy-start.4 = (s32[128]{0:T(128)S(1)}, s32[128]{0:T(128)}, u32[]{:S(2)}) copy-start(s32[128]{0:T(128)} %param.14) | copy-start | bytes 1540
  7.2 13.4 %copy-start.7 = (s32[128]{0:T(128)S(1)}, s32[128]{0:T(128)}, u32[]{:S(2)}) copy-start(s32[128]{0:T(128)} %param.15) | copy-start | bytes 1540
  7.2 13.7 %copy-start.6 = (f32[16,64]{1,0:T(8,128)S(1)}, f32[16,64]{1,0:T(8,128)}, u32[]{:S(2)}) copy-start(f32[16,64]{1,0:T(8,128)} %param.13) | copy-start | bytes 12292
  7.2 25.8 %all-gather.2.cloned.1.call-start = ((), (), s32[]{:S(2)}) async-start(), calls=%async_computation.2 | async-start | bytes 9830400 | tf_op jit(solution)/shard_map/all_gather | solution.py:33
  10.2 11.0 %copy-start.3 = (s32[1024]{0:T(1024)}, s32[1024]{0:T(1024)S(1)}, u32[]{:S(2)}) copy-start(s32[1024]{0:T(1024)S(1)} %pad_clamp_fusion) | copy-start | bytes 12292
  12.2 42.4 %all-to-all-start = ((f32[16,8,1]{1,2,0:T(1,128)}), f32[16,8,1]{1,2,0:T(1,128)S(1)}, u32[]{:S(2)}, u32[]{:S(2)}) async-start(f32[16,8,1]{1,2,0:T(1,128)} %bitcast.4), calls=%async_computation | async-start | bytes 16384 | tf_op jit(solution)/shard_map/all_to_all | solution.py:81
  20.5 143.9 %all-reduce.3.cloned.1.call-start = ((), (), s32[]{:S(2)}) async-start(), calls=%async_computation.3 | async-start | bytes 655360
  33.0 9.6 %copy-start.2 = (f32[128,1,50]{1,2,0:T(8,128)S(1)}, f32[128,1,50]{1,2,0:T(8,128)}, u32[]{:S(2)}) copy-start(f32[128,1,50]{1,2,0:T(8,128)} %fusion.2) | copy-start | bytes 76804
  49.1 1.7 copy-start.5
  54.6 14.7 %all-to-all-start.1 = ((f32[16,8,256]{2,1,0:T(8,128)}), f32[16,8,256]{2,1,0:T(8,128)S(1)}, u32[]{:S(2)}, u32[]{:S(2)}) async-start(f32[16,8,256]{2,1,0:T(8,128)} %bitcast.6), calls=%async_computation.1 | async-start | bytes 262144 | tf_op jit(solution)/shard_map/all_to_all | solution.py:80
Sparse Core Ops, SparseCore 0:
  9.6 19.8 all-gather.1
  54.7 109.7 all-reduce.2
where the time goes:
time: 175 us; the launch traced here: 174 us
  waiting for transfers between devices  102 us (58%)
  matrix products  18.1 us (10%)
  local copies, waits for them, and re-layouts  15.7 us (9%)
  starting transfers between devices  15.3 us (9%)
  between operations  14.3 us (8%)
  other arithmetic  8.96 us (5%)
    unnamed x3, waiting for transfers between devices  94.2 us
    dot_general x1, matrix products, pulsar_terms(): jnp.einsum('tkr,tjr->tkj', lax.all_gather(basis_own, 'rep', axis=1, tiled...  9.59 us
    all_to_all x1, starting transfers between devices, shards(): lax.all_to_all(place_float, 'toa', split_axis=0, concat_axis=0, tiled=True)  8.34 us
    all_to_all x1, waiting for transfers between devices, shards(): lax.all_to_all(whitened_local[send_order], 'toa', split_axis=0, concat_ax...  7.67 us
    all_to_all x1, starting transfers between devices, shards(): lax.all_to_all(whitened_local[send_order], 'toa', split_axis=0, concat_ax...  6.91 us
    broadcast_in_dim x1, matrix products, pulsar_terms(): tile_proj[:, None, :]  4.14 us
    dot_general x1, matrix products, pulsar_terms(): jnp.dot(onehot_pulsar.T, stacked, precision=lax.Precision.HIGHEST)  3.8 us
    concatenate x1, local copies, waits for them, and re-layouts, pulsar_terms(): jnp.concatenate([tile_gram, tile_proj[:, None, :]], axis=1)  3.66 us
  transfers between devices with their start and end apart: 4, of which 2 were waited for; matrix products, arithmetic and copies ran while one was open for 23% of the time, Pallas kernels for 0%

commit v1 on v0

v1 whole, which is shorter than its diff:
```python
import functools

import jax
import jax.numpy as jnp
from jax import lax
from jax.experimental import pallas as pl
from jax.experimental.pallas import tpu as pltpu
from jax.sharding import PartitionSpec as P

MESH = pl.DeviceIdType.MESH
GROUP = 16
LANES = 128


def round_up(value, step):
    return (value + step - 1) // step * step


def local_kernel(
    peers,
    pulsar_ref,
    backend_ref,
    counts_ref,
    slot_ref,
    efac_ref,
    equad_ref,
    residual_ref,
    error_ref,
    own_ref,
    other_ref,
    rows_ref,
    part_ref,
    total,
    filled,
):
    step = pl.program_id(0)
    half, group, row_total = own_ref.shape
    pulsar_total = total.shape[0]
    tile_total = group * pl.num_programs(0)
    per_peer = tile_total // peers

    @pl.when(step == 0)
    def _():
        total[...] = jnp.zeros_like(total)

        def clear(i, carry):
            filled[i] = 0
            return carry

        lax.fori_loop(0, peers, clear, 0)

    def tiles_first(ref):
        block = ref[...].astype(jnp.float32)
        block = jnp.concatenate(
            [block, jnp.zeros((round_up(half + 2, 8) - half, group, row_total), jnp.float32)], axis=0
        )
        return jnp.swapaxes(block, 0, 1)

    own = tiles_first(own_ref)
    other = tiles_first(other_ref)
    lane = lax.broadcasted_iota(jnp.int32, (1, row_total), 1)
    below = lax.broadcasted_iota(jnp.int32, (own.shape[1], row_total), 0)
    for i in range(group):
        tile = step * group + i
        p = pulsar_ref[tile]
        b = backend_ref[tile]
        factor = efac_ref[p, b]
        floor_term = equad_ref[p, b]
        residual = residual_ref[i : i + 1, :]
        error = error_ref[i : i + 1, :]
        weight = jnp.where(
            lane < counts_ref[tile],
            1.0 / (factor * factor * (error * error) + floor_term * floor_term),
            0.0,
        )
        slot = slot_ref[tile]
        dest = slot // tile_total
        rank = filled[dest]
        filled[dest] = rank + 1
        place = (slot - dest * tile_total).astype(jnp.float32)
        position = dest * per_peer + rank
        white = jnp.sqrt(weight) * residual
        for c in range(row_total // LANES):
            rows_ref[position, c : c + 1, :] = white[:, c * LANES : (c + 1) * LANES]
        rows_ref[position, row_total // LANES :, :] = jnp.full((1, LANES), place, jnp.float32)
        basis = own[i]
        left = jnp.where(below == half, weight * residual, weight * basis).astype(jnp.bfloat16)
        right = jnp.concatenate([basis, other[i]], axis=0).astype(jnp.bfloat16)
        gram = lax.dot_general(
            left, right, (((1,), (1,)), ((), ())), preferred_element_type=jnp.float32
        )
        total[p] += gram

    @pl.when(step == pl.num_programs(0) - 1)
    def _():
        def narrow(q, carry):
            block = total[q]
            high = block.astype(jnp.bfloat16)
            rest = block - high.astype(jnp.float32)
            index = lax.broadcasted_iota(jnp.int32, block.shape, 0)
            shifted = pltpu.roll(rest, 1, 0)
            part_ref[q] = jnp.where(index == half + 1, shifted, high.astype(jnp.float32)).astype(
                jnp.bfloat16
            )
            return carry

        lax.fori_loop(0, pulsar_total, narrow, 0)


def exchange_kernel(
    peers,
    half,
    rows_ref,
    part_ref,
    white_ref,
    gram_ref,
    got_rows,
    got_part,
    sends,
    arrivals,
):
    me = lax.axis_index("toa")
    owned = part_ref.shape[0] // peers
    tile_total = white_ref.shape[0]
    row_total = white_ref.shape[1]
    barrier = pltpu.get_barrier_semaphore()
    for d in range(1, peers):
        pl.semaphore_signal(
            barrier, inc=1, device_id={"toa": lax.rem(me + d, peers)}, device_id_type=MESH
        )
    pl.semaphore_wait(barrier, peers - 1)

    def copies(d):
        peer = lax.rem(me + d, peers)
        first = pltpu.make_async_remote_copy(
            src_ref=part_ref.at[pl.ds(peer * owned, owned)],
            dst_ref=got_part.at[d],
            send_sem=sends.at[0, d],
            recv_sem=arrivals.at[0, d],
            device_id={"toa": peer},
            device_id_type=MESH,
        )
        second = pltpu.make_async_remote_copy(
            src_ref=rows_ref.at[peer],
            dst_ref=got_rows.at[d],
            send_sem=sends.at[1, d],
            recv_sem=arrivals.at[1, d],
            device_id={"toa": peer},
            device_id_type=MESH,
        )
        return (first, second)

    def start(d, carry):
        for copy in copies(d):
            copy.start()
        return carry

    def finish(d, carry):
        for copy in copies(d):
            copy.wait()
        return carry

    lax.fori_loop(1, peers, start, 0)
    got_rows[0] = rows_ref[me]
    got_part[0] = part_ref[pl.ds(me * owned, owned)]
    lax.fori_loop(1, peers, finish, 0)

    summed = lax.fori_loop(
        0,
        peers,
        lambda d, acc: acc + got_part[d].astype(jnp.float32),
        jnp.zeros(got_part.shape[1:], jnp.float32),
    )
    gram_ref[...] = summed
    chunks = row_total // LANES
    places = got_rows[:, :, chunks, :].reshape(tile_total, LANES)
    data = jnp.concatenate(
        [got_rows[:, :, c, :].reshape(tile_total, LANES) for c in range(chunks)], axis=1
    )
    for first in range(0, tile_total, LANES):
        spot = first + lax.broadcasted_iota(jnp.int32, (tile_total, LANES), 1)
        chosen = (places == spot.astype(jnp.float32)).astype(jnp.float32)
        white_ref[first : first + LANES, :] = lax.dot_general(
            chosen,
            data,
            (((0,), (0,)), ((), ())),
            precision=lax.Precision.HIGHEST,
            preferred_element_type=jnp.float32,
        )


def shards(
    residual, toa_error, basis_rows, efac_table, equad_table, pulsar, backend, counts, owner_slot
):
    tile_total, row_total = residual.shape
    peers = lax.axis_size("toa")
    half = basis_rows.shape[1]
    pulsar_total = efac_table.shape[0]
    owned = pulsar_total // peers
    per_peer = tile_total // peers
    padded = round_up(half + 2, 8)
    pieces = row_total // LANES + 1
    group = min(GROUP, tile_total)
    own = jnp.transpose(basis_rows, (1, 0, 2))
    other = lax.ppermute(own, "rep", [(0, 1), (1, 0)])
    smem = pl.BlockSpec(memory_space=pltpu.SMEM)
    rows, parts = pl.pallas_call(
        functools.partial(local_kernel, peers),
        grid=(tile_total // group,),
        in_specs=[smem] * 6
        + [pl.BlockSpec((group, row_total), lambda i: (i, 0))] * 2
        + [pl.BlockSpec((half, group, row_total), lambda i: (0, i, 0))] * 2,
        out_specs=[
            pl.BlockSpec((tile_total, pieces, LANES), lambda i: (0, 0, 0)),
            pl.BlockSpec((pulsar_total, padded, 2 * padded), lambda i: (0, 0, 0)),
        ],
        out_shape=[
            jax.ShapeDtypeStruct((tile_total, pieces, LANES), jnp.float32),
            jax.ShapeDtypeStruct((pulsar_total, padded, 2 * padded), jnp.bfloat16),
        ],
        scratch_shapes=[
            pltpu.VMEM((pulsar_total, padded, 2 * padded), jnp.float32),
            pltpu.SMEM((peers,), jnp.int32),
        ],
        name="local_terms",
    )(
        pulsar,
        backend,
        counts,
        owner_slot,
        efac_table,
        equad_table,
        residual,
        toa_error,
        own,
        other,
    )
    vmem = pl.BlockSpec(memory_space=pltpu.VMEM)
    whitened, summed = pl.pallas_call(
        functools.partial(exchange_kernel, peers, half),
        in_specs=[vmem] * 2,
        out_specs=[vmem] * 2,
        out_shape=[
            jax.ShapeDtypeStruct((tile_total, row_total), jnp.float32),
            jax.ShapeDtypeStruct((owned, padded, 2 * padded), jnp.float32),
        ],
        scratch_shapes=[
            pltpu.VMEM((peers, per_peer, pieces, LANES), jnp.float32),
            pltpu.VMEM((peers, owned, padded, 2 * padded), jnp.bfloat16),
            pltpu.SemaphoreType.DMA((2, peers)),
            pltpu.SemaphoreType.DMA((2, peers)),
        ],
        compiler_params=pltpu.CompilerParams(collective_id=0, has_side_effects=True),
        name="exchange",
    )(rows.reshape(peers, per_peer, pieces, LANES), parts)
    projection = summed[:, half, :half] + summed[:, half + 1, :half]
    mine = summed[:, :half, :half]
    theirs = summed[:, :half, padded : padded + half]
    first_core = lax.axis_index("rep") == 0
    gram = jnp.concatenate(
        [jnp.where(first_core, mine, theirs), jnp.where(first_core, theirs, mine)], axis=2
    )
    return (jnp.transpose(gram, (0, 2, 1)), projection, whitened)


def solution(mesh):
    in_specs = (
        P("toa", None),
        P("toa", None),
        P("toa", "rep", None),
        P(),
        P(),
        P("toa"),
        P("toa"),
        P("toa"),
        P("toa"),
    )
    out_specs = (P("toa", None, "rep"), P("toa", "rep"), P("toa", None))
    return jax.shard_map(shards, mesh=mesh, in_specs=in_specs, out_specs=out_specs, check_vma=False)
```

time: 175 us -> 40.8 us (0.23)
  the two profiles are of different devices: /device:TPU:0 before, /device:TPU:15 now
where the time goes in v1:
time: 40.8 us; the launch traced here: 40.4 us
  Pallas kernels  27.2 us (67%)
  waiting for transfers between devices  5.68 us (14%)
  local copies, waits for them, and re-layouts  3.87 us (9%)
  other arithmetic  2.25 us (6%)
  starting transfers between devices  0.74 us (2%)
  between operations  0.65 us (2%)
    pallas_call x1, Pallas kernels, shards(): pl.pallas_call(functools.partial(exchange_kernel, peers, half), in_specs=...  17.4 us
    pallas_call x1, Pallas kernels, shards(): pl.pallas_call(functools.partial(local_kernel, peers), grid=(tile_total /...  9.85 us
    ppermute x1, waiting for transfers between devices, shards(): other = lax.ppermute(own, 'rep', [(0, 1), (1, 0)])  5.68 us
    unnamed x4, local copies, waits for them, and re-layouts  3.87 us
    add x1, other arithmetic, shards(): projection = summed[:, half, :half] + summed[:, half + 1, :half]  1.27 us
    select_n x1, other arithmetic, shards(): jnp.where(first_core, mine, theirs)  0.9 us
  transfers between devices with their start and end apart: 1, of which 1 were waited for; matrix products, arithmetic and copies ran while one was open for 0% of the time, Pallas kernels for 0%

profile of v1, /device:TPU:15, one launch (start us, length us, event | category | flops | bytes accessed | tf_op | source)
XLA Modules:
  0.0 40.4 jit_solution(8178485270174384550)
XLA Ops:
  0.6 0.7 %collective-permute-start = (bf16[50,128,256]{2,1,0:T(8,128)(2,1)}, bf16[50,128,256]{2,1,0:T(8,128)(2,1)S(1)}, u32[]{:S(2)}, u32[]{:S(2)}) collective-permute-start(bf16[50,128,256]{2,1,0:T(8,128)(2,1)} %bitcast.6), channel_id=1, source_target_pairs={{0,1},{1,0},{2,3},{3,2},{4,5},{5,4},{6,7},{7,6},{8,9},{9,8},{10,11... | collective-permute-start | bytes 9830408 | tf_op jit(solution)/shard_map/ppermute | solution.py:205
  1.4 5.7 %collective-permute-done.other_ref = bf16[50,128,256]{2,1,0:T(8,128)(2,1)S(1)} collective-permute-done((bf16[50,128,256]{2,1,0:T(8,128)(2,1)}, bf16[50,128,256]{2,1,0:T(8,128)(2,1)S(1)}, u32[]{:S(2)}, u32[]{:S(2)}) %collective-permute-start) | collective-permute-done | bytes 3276832 | tf_op jit(solution)/shard_map/ppermute | solution.py:205
  7.1 0.0 copy-start
  7.1 1.7 %copy-done = bf16[50,128,256]{2,1,0:T(8,128)(2,1)} copy-done((bf16[50,128,256]{2,1,0:T(8,128)(2,1)}, bf16[50,128,256]{2,1,0:T(8,128)(2,1)S(1)}, u32[]{:S(2)}) %copy-start) | copy-done | bytes 3276824
  8.7 9.8 %local_terms.1 = (f32[128,3,128]{2,1,0:T(4,128)}, bf16[16,56,112]{2,1,0:T(8,128)(2,1)}) custom-call(s32[128]{0:T(128)} %pulsar_ref.1, s32[128]{0:T(128)} %backend_ref.1, s32[128]{0:T(128)} %counts_ref.1, s32[128]{0:T(128)} %slot_ref.1, f32[16,64]{1,0:T(8,128)} %efac_ref.1, f32[16,64]{1,0:T(8,128)} %equad_ref.1, f32[128,256]{1,0:T(8,128)} %residual_ref.1, ...), custom_call_target="tpu_custom_call" | custom-call | tf_op jit(solution)/shard_map/local_terms/pallas_call | solution.py:207
  18.6 17.4 %exchange.1 = (f32[128,256]{1,0:T(8,128)}, f32[1,56,112]{2,1,0:T(8,128)}) custom-call(f32[16,8,3,128]{3,2,1,0:T(4,128)} %bitcast.8, bf16[16,56,112]{2,1,0:T(8,128)(2,1)} %get-tuple-element.8.part_ref), custom_call_target="tpu_custom_call" | custom-call | tf_op jit(solution)/shard_map/exchange/pallas_call | solution.py:239
  36.0 1.3 %add_bitcast_fusion = f32[1,50]{1,0:T(1,128)} fusion(f32[1,56,112]{2,1,0:T(8,128)} %get-tuple-element.9), kind=kLoop, calls=%fused_computation.3 | loop fusion | flops 50 | bytes 600 | tf_op jit(solution)/shard_map/add | solution.py:256
  37.2 0.9 %slice_select_fusion.1 = (f32[1,50,50]{2,1,0:T(8,128)S(1)}, f32[1,50,50]{2,1,0:T(8,128)S(1)}) fusion(f32[1,56,112]{2,1,0:T(8,128)} %get-tuple-element.9, pred[]{:T(512)S(6)} %eq.3), kind=kLoop, calls=%fused_computation.2 | loop fusion | flops 5000 | bytes 40001 | tf_op jit(solution)/shard_map/jit(_where)/select_n | solution.py:261
  38.1 0.1 maximum_bitcast_fusion
  38.2 0.6 %copy.12 = f32[1,100,50]{1,0,2:T(1,128)} copy(f32[1,100,50]{1,2,0:T(8,128)S(1)} %maximum_bitcast_fusion) | data formatting | bytes 40000
  38.8 1.6 %copy.14 = f32[128,256]{1,0:T(8,128)} copy(f32[128,256]{1,0:T(8,128)} %get-tuple-element.21) | data formatting | bytes 262144
Async XLA Ops:
  0.6 6.4 %collective-permute-start = (bf16[50,128,256]{2,1,0:T(8,128)(2,1)}, bf16[50,128,256]{2,1,0:T(8,128)(2,1)S(1)}, u32[]{:S(2)}, u32[]{:S(2)}) collective-permute-start(bf16[50,128,256]{2,1,0:T(8,128)(2,1)} %bitcast.6), channel_id=1, source_target_pairs={{0,1},{1,0},{2,3},{3,2},{4,5},{5,4},{6,7},{7,6},{8,9},{9,8},{10,11... | collective-permute-start | bytes 9830408 | tf_op jit(solution)/shard_map/ppermute | solution.py:205
  7.1 1.7 %copy-start = (bf16[50,128,256]{2,1,0:T(8,128)(2,1)}, bf16[50,128,256]{2,1,0:T(8,128)(2,1)S(1)}, u32[]{:S(2)}) copy-start(bf16[50,128,256]{2,1,0:T(8,128)(2,1)S(1)} %collective-permute-done.other_ref) | copy-start | bytes 9830404

commit v2 on v0

v2 whole, which is shorter than its diff:
```python
import functools

import jax
import jax.numpy as jnp
from jax import lax
from jax.experimental import pallas as pl
from jax.experimental.pallas import tpu as pltpu
from jax.sharding import PartitionSpec as P

MESH = pl.DeviceIdType.MESH
GROUP = 16
LANES = 128
VMEM_ALL = 67043328
HIGH = lax.Precision.HIGHEST


def round_up(value, step):
    return (value + step - 1) // step * step


def meet(peers, me):
    barrier = pltpu.get_barrier_semaphore()

    def greet(d, carry):
        pl.semaphore_signal(
            barrier, inc=1, device_id={"toa": lax.rem(me + d, peers)}, device_id_type=MESH
        )
        return carry

    lax.fori_loop(1, peers, greet, 0)
    return barrier


def contract(left, right, dims, precision=None):
    return lax.dot_general(
        left, right, (dims, ((), ())), precision=precision, preferred_element_type=jnp.float32
    )


def spread_kernel(
    peers,
    pulsar_ref,
    backend_ref,
    counts_ref,
    slot_ref,
    efac_ref,
    equad_ref,
    residual_ref,
    error_ref,
    weight_ref,
    got_rows,
    got_places,
    sorted_rows,
    sorted_places,
    sends,
    arrivals,
    local_sem,
):
    me = lax.axis_index("toa")
    barrier = meet(peers, me)
    tile_total, row_total = residual_ref.shape
    per_peer = tile_total // peers

    def onehot(row, amount):
        index = lax.broadcasted_iota(jnp.int32, (amount, tile_total), 0)
        return (index == row).astype(jnp.float32)

    pulsar_hot = onehot(pulsar_ref[...], efac_ref.shape[0])
    backend_hot = onehot(backend_ref[...], efac_ref.shape[1])

    def lookup(ref):
        columns = contract(ref[...], pulsar_hot, ((0,), (0,)), HIGH)
        return jnp.sum(columns * backend_hot, axis=0, keepdims=True)

    factor = lookup(efac_ref)
    floor_term = lookup(equad_ref)
    slot = slot_ref[...]
    dest = slot // tile_total
    place = (slot - dest * tile_total).astype(jnp.float32)
    dest_hot = onehot(dest, peers)
    earlier = (
        lax.broadcasted_iota(jnp.int32, (tile_total, tile_total), 0)
        < lax.broadcasted_iota(jnp.int32, (tile_total, tile_total), 1)
    ).astype(jnp.float32)
    before = contract(dest_hot, earlier, ((1,), (0,)), HIGH)
    rank = jnp.sum(before * dest_hot, axis=0, keepdims=True)
    position = dest * per_peer + rank.astype(jnp.int32)
    order = onehot(position, tile_total)
    stacked = jnp.concatenate(
        [
            factor * factor,
            floor_term * floor_term,
            counts_ref[...].astype(jnp.float32),
            place,
            jnp.zeros((tile_total - 4, tile_total), jnp.float32),
        ],
        axis=0,
    )
    columns = jnp.transpose(stacked)
    lane = lax.broadcasted_iota(jnp.int32, (tile_total, row_total), 1).astype(jnp.float32)
    error = error_ref[...]
    weight = jnp.where(
        lane < columns[:, 2:3], 1.0 / (columns[:, 0:1] * (error * error) + columns[:, 1:2]), 0.0
    )
    weight_ref[...] = weight
    white = jnp.sqrt(weight) * residual_ref[...]
    sorted_rows[...] = contract(order, white, ((1,), (0,)), HIGH).reshape(sorted_rows.shape)
    sorted_places[...] = contract(place, order, ((1,), (1,)), HIGH).astype(jnp.int32)
    own_rows = pltpu.make_async_copy(sorted_rows.at[me], got_rows.at[0], local_sem.at[0])
    own_places = pltpu.make_async_copy(sorted_places, got_places.at[0], local_sem.at[1])
    own_rows.start()
    own_places.start()
    pl.semaphore_wait(barrier, peers - 1)

    def copies(d):
        peer = lax.rem(me + d, peers)
        pairs = ((sorted_rows.at[peer], got_rows.at[d]), (sorted_places, got_places.at[d]))
        return [
            pltpu.make_async_remote_copy(
                src_ref=source,
                dst_ref=target,
                send_sem=sends.at[n, d],
                recv_sem=arrivals.at[n, d],
                device_id={"toa": peer},
                device_id_type=MESH,
            )
            for n, (source, target) in enumerate(pairs)
        ]

    def start(d, carry):
        for copy in copies(d):
            copy.start()
        return carry

    def finish(d, carry):
        for copy in copies(d):
            copy.wait()
        return carry

    lax.fori_loop(1, peers, start, 0)
    own_rows.wait()
    own_places.wait()
    lax.fori_loop(1, peers, finish, 0)


def local_kernel(
    peers,
    pulsar_ref,
    places_ref,
    weight_ref,
    residual_ref,
    own_ref,
    other_ref,
    rows_ref,
    part_ref,
    white_ref,
    total,
    staged,
):
    step = pl.program_id(0)
    half, group, row_total = own_ref.shape
    pulsar_total, padded, width = total.shape
    me = lax.axis_index("toa")
    per_peer = rows_ref.shape[1]

    @pl.when(step == 0)
    def _():
        total[...] = jnp.zeros_like(total)

    def tiles_first(ref):
        block = ref[...].astype(jnp.float32)
        block = jnp.concatenate(
            [block, jnp.zeros((padded - half, group, row_total), jnp.float32)], axis=0
        )
        return jnp.swapaxes(block, 0, 1)

    own = tiles_first(own_ref)
    other = tiles_first(other_ref)
    below = lax.broadcasted_iota(jnp.int32, (padded, row_total), 0)
    for i in range(group):
        p = pulsar_ref[step * group + i]
        weight = weight_ref[i : i + 1, :]
        basis = own[i]
        left = jnp.where(below == half, residual_ref[i : i + 1, :], basis)
        left = (weight * left).astype(jnp.bfloat16)
        right = jnp.concatenate([basis, other[i]], axis=0).astype(jnp.bfloat16)
        total[p] += contract(left, right, ((1,), (1,)))

    source = step * (peers // pl.num_programs(0)) if peers % pl.num_programs(0) == 0 else None
    sources = range(peers // pl.num_programs(0)) if source is not None else ()

    def settle(d):
        for i in range(per_peer):
            place = places_ref[d, 0, me * per_peer + i]
            for c in range(row_total // LANES):
                staged[c, pl.ds(place, 1), :] = rows_ref[d, i : i + 1, c * LANES : (c + 1) * LANES]

    for s in sources:
        settle(source + s)

    @pl.when(step == pl.num_programs(0) - 1)
    def _():
        if source is None:

            def settle_one(d, carry):
                settle(d)
                return carry

            lax.fori_loop(0, peers, settle_one, 0)
        for c in range(row_total // LANES):
            white_ref[:, c * LANES : (c + 1) * LANES] = staged[c]

        def narrow(q, carry):
            block = total[q]
            high = block.astype(jnp.bfloat16).astype(jnp.float32)
            index = lax.broadcasted_iota(jnp.int32, block.shape, 0)
            shifted = pltpu.roll(block - high, 1, 0)
            part_ref[q] = jnp.where(index == half + 1, shifted, high).astype(jnp.bfloat16)
            return carry

        lax.fori_loop(0, pulsar_total, narrow, 0)


def gather_kernel(peers, part_ref, sum_ref, got_part, sends, arrivals):
    me = lax.axis_index("toa")
    owned = part_ref.shape[0] // peers
    barrier = meet(peers, me)
    pl.semaphore_wait(barrier, peers - 1)

    def copy_to(d):
        peer = lax.rem(me + d, peers)
        return pltpu.make_async_remote_copy(
            src_ref=part_ref.at[pl.ds(peer * owned, owned)],
            dst_ref=got_part.at[d],
            send_sem=sends.at[d],
            recv_sem=arrivals.at[d],
            device_id={"toa": peer},
            device_id_type=MESH,
        )

    def start(d, carry):
        copy_to(d).start()
        return carry

    def take(d, acc):
        copy_to(d).wait()
        return acc + got_part[d].astype(jnp.float32)

    lax.fori_loop(1, peers, start, 0)
    mine = part_ref[pl.ds(me * owned, owned)].astype(jnp.float32)
    sum_ref[...] = lax.fori_loop(1, peers, take, mine)


def finish_kernel(half, sum_ref, gram_ref, projection_ref):
    first_core = lax.axis_index("rep") == 0
    padded = sum_ref.shape[1]
    for q in range(sum_ref.shape[0]):
        block = sum_ref[q]
        projection_ref[q : q + 1, :] = (
            block[half : half + 1, :half] + block[half + 1 : half + 2, :half]
        )
        mine = block[:half, :half]
        theirs = block[:half, padded : padded + half]
        gram_ref[:, q, :half] = jnp.where(first_core, mine, theirs)
        gram_ref[:, q, half:] = jnp.where(first_core, theirs, mine)


def shards(
    residual, toa_error, basis_rows, efac_table, equad_table, pulsar, backend, counts, owner_slot
):
    tile_total, row_total = residual.shape
    peers = lax.axis_size("toa")
    half = basis_rows.shape[1]
    pulsar_total = efac_table.shape[0]
    owned = pulsar_total // peers
    per_peer = tile_total // peers
    padded = round_up(half + 2, 8)
    width = 2 * padded
    group = min(GROUP, tile_total)
    steps = tile_total // group
    chunks = row_total // LANES
    f32 = jnp.float32
    smem = pl.BlockSpec(memory_space=pltpu.SMEM)
    vmem = pl.BlockSpec(memory_space=pltpu.VMEM)
    own = jnp.transpose(basis_rows, (1, 0, 2))
    other = lax.ppermute(own, "rep", [(0, 1), (1, 0)])

    def row(vector):
        return vector.reshape(1, tile_total)

    weight, rows, places = pl.pallas_call(
        functools.partial(spread_kernel, peers),
        in_specs=[vmem] * 8,
        out_specs=[vmem] * 3,
        out_shape=[
            jax.ShapeDtypeStruct((tile_total, row_total), f32),
            jax.ShapeDtypeStruct((peers, per_peer, row_total), f32),
            jax.ShapeDtypeStruct((peers, 1, tile_total), jnp.int32),
        ],
        scratch_shapes=[
            pltpu.VMEM((peers, per_peer, row_total), f32),
            pltpu.VMEM((1, tile_total), jnp.int32),
            pltpu.SemaphoreType.DMA((2, peers)),
            pltpu.SemaphoreType.DMA((2, peers)),
            pltpu.SemaphoreType.DMA((2,)),
        ],
        compiler_params=pltpu.CompilerParams(collective_id=1, has_side_effects=True),
        cost_estimate=pl.CostEstimate(
            flops=16 * tile_total * tile_total * row_total,
            bytes_accessed=5 * 4 * tile_total * row_total,
            transcendentals=tile_total * row_total,
        ),
        name="spread",
    )(
        row(pulsar),
        row(backend),
        row(counts),
        row(owner_slot),
        efac_table,
        equad_table,
        residual,
        toa_error,
    )
    parts, whitened = pl.pallas_call(
        functools.partial(local_kernel, peers),
        grid=(steps,),
        in_specs=[smem] * 2
        + [pl.BlockSpec((group, row_total), lambda i: (i, 0))] * 2
        + [pl.BlockSpec((half, group, row_total), lambda i: (0, i, 0))] * 2
        + [pl.BlockSpec((peers, per_peer, row_total), lambda i: (0, 0, 0))],
        out_specs=[
            pl.BlockSpec((pulsar_total, padded, width), lambda i: (0, 0, 0)),
            pl.BlockSpec((tile_total, row_total), lambda i: (0, 0)),
        ],
        out_shape=[
            jax.ShapeDtypeStruct((pulsar_total, padded, width), jnp.bfloat16),
            jax.ShapeDtypeStruct((tile_total, row_total), f32),
        ],
        scratch_shapes=[
            pltpu.VMEM((pulsar_total, padded, width), f32),
            pltpu.VMEM((chunks, tile_total, LANES), f32),
        ],
        compiler_params=pltpu.CompilerParams(vmem_limit_bytes=VMEM_ALL),
        name="local_terms",
    )(pulsar, places, weight, residual, own, other, rows)
    summed = pl.pallas_call(
        functools.partial(gather_kernel, peers),
        in_specs=[vmem],
        out_specs=vmem,
        out_shape=jax.ShapeDtypeStruct((owned, padded, width), f32),
        scratch_shapes=[
            pltpu.VMEM((peers, owned, padded, width), jnp.bfloat16),
            pltpu.SemaphoreType.DMA((peers,)),
            pltpu.SemaphoreType.DMA((peers,)),
        ],
        compiler_params=pltpu.CompilerParams(collective_id=0, has_side_effects=True),
        name="gather_parts",
    )(parts)
    gram, projection = pl.pallas_call(
        functools.partial(finish_kernel, half),
        in_specs=[vmem],
        out_specs=[vmem] * 2,
        out_shape=[
            jax.ShapeDtypeStruct((half, owned, 2 * half), f32),
            jax.ShapeDtypeStruct((owned, half), f32),
        ],
        name="finish",
    )(summed)
    return (jnp.transpose(gram, (1, 2, 0)), projection, whitened)


def solution(mesh):
    in_specs = (
        P("toa", None),
        P("toa", None),
        P("toa", "rep", None),
        P(),
        P(),
        P("toa"),
        P("toa"),
        P("toa"),
        P("toa"),
    )
    out_specs = (P("toa", None, "rep"), P("toa", "rep"), P("toa", None))
    return jax.shard_map(shards, mesh=mesh, in_specs=in_specs, out_specs=out_specs, check_vma=False)
```

time: 175 us -> 35.7 us (0.20)
  waiting for transfers between devices: 102 us -> 0.01 us
  Pallas kernels: 0 us -> 34.1 us
  matrix products: 18.1 us -> 0 us
  local copies, waits for them, and re-layouts: 15.7 us -> 0 us
  starting transfers between devices: 15.3 us -> 0.56 us
  between operations: 14.3 us -> 0.66 us
  other arithmetic: 8.96 us -> 0 us
    unnamed x3 -> x0, waiting for transfers between devices: 94.2 us -> none
    pallas_call x0 -> x4, Pallas kernels: none -> 34.1 us  [the longest x1 12.1 us: shards(): pl.pallas_call(functools.partial(spread_kernel, peers), in_specs=[vmem] *...]
    all_to_all x2 -> x0, starting transfers between devices: 15.3 us -> none  [the longest x1 8.34 us: shards(): lax.all_to_all(place_float, 'toa', split_axis=0, concat_axis=0, tiled=True)]
    dot_general x4 -> x0, matrix products: 13.9 us -> none  [the longest x1 9.59 us: pulsar_terms(): jnp.einsum('tkr,tjr->tkj', lax.all_gather(basis_own, 'rep', axis=1, tiled...]
    all_to_all x2 -> x0, waiting for transfers between devices: 7.67 us -> none  [the longest x1 7.67 us: shards(): lax.all_to_all(whitened_local[send_order], 'toa', split_axis=0, concat_ax...]
    broadcast_in_dim x1 -> x0, matrix products: 4.14 us -> none  [pulsar_terms(): tile_proj[:, None, :]]
    convert_element_type x5 -> x0, other arithmetic: 3.76 us -> none  [the longest x1 2.68 us: pulsar_terms(): scaled = (weight[:, None, :] * basis_own).astype(jnp.bfloat16)]
    concatenate x1 -> x0, local copies, waits for them, and re-layouts: 3.66 us -> none  [pulsar_terms(): jnp.concatenate([tile_gram, tile_proj[:, None, :]], axis=1)]
  transfers between devices with their start and end apart: 4 -> 1, of which waited for: 2 -> 0; matrix products, arithmetic and copies ran while one was open for 23% -> 0% of each run, Pallas kernels for 0% -> 34%
where the time goes in v2:
time: 35.7 us; the launch traced here: 35.3 us
  Pallas kernels  34.1 us (96%)
  between operations  0.66 us (2%)
  starting transfers between devices  0.56 us (2%)
    pallas_call x1, Pallas kernels, shards(): pl.pallas_call(functools.partial(spread_kernel, peers), in_specs=[vmem] *...  12.1 us
    pallas_call x1, Pallas kernels, shards(): pl.pallas_call(functools.partial(gather_kernel, peers), in_specs=[vmem],...  11.1 us
    pallas_call x1, Pallas kernels, shards(): pl.pallas_call(functools.partial(local_kernel, peers), grid=(steps,), in_...  9.38 us
    pallas_call x1, Pallas kernels, shards(): pl.pallas_call(functools.partial(finish_kernel, half), in_specs=[vmem], o...  1.55 us
  transfers between devices with their start and end apart: 1, of which 0 were waited for; matrix products, arithmetic and copies ran while one was open for 0% of the time, Pallas kernels for 34%

profile of v2, /device:TPU:0, one launch (start us, length us, event | category | flops | bytes accessed | tf_op | source)
XLA Modules:
  0.0 35.3 jit_solution(6594800596269166671)
XLA Ops:
  0.6 0.6 %collective-permute-start = (bf16[50,128,256]{2,1,0:T(8,128)(2,1)}, bf16[50,128,256]{2,1,0:T(8,128)(2,1)}, u32[]{:S(2)}, u32[]{:S(2)}) collective-permute-start(bf16[50,128,256]{2,1,0:T(8,128)(2,1)} %bitcast.6), channel_id=1, source_target_pairs={{0,1},{1,0},{2,3},{3,2},{4,5},{5,4},{6,7},{7,6},{8,9},{9,8},{10,11... | collective-permute-start | bytes 9830408 | tf_op jit(solution)/shard_map/ppermute | solution.py:286
  1.2 12.1 %spread.1 = (f32[128,256]{1,0:T(8,128)}, f32[16,8,256]{2,1,0:T(8,128)}, s32[16,1,128]{2,1,0:T(1,128)}) custom-call(s32[1,128]{1,0:T(1,128)} %bitcast.8, s32[1,128]{1,0:T(1,128)} %bitcast.9, s32[1,128]{1,0:T(1,128)} %bitcast.10, s32[1,128]{1,0:T(1,128)} %bitcast.11, f32[16,64]{1,0:T(8,128)} %efac_ref.1, f32[16,64]{1,0:T(8,128)} %equad_ref.1, ...), custom_call_target="tpu_custom_call" | custom-call | flops 67108864 | bytes 655360 | tf_op jit(solution)/shard_map/spread/pallas_call | solution.py:291
  13.3 0.0 collective-permute-done.other_ref
  13.3 9.4 %local_terms.1 = (bf16[16,56,112]{2,1,0:T(8,128)(2,1)}, f32[128,256]{1,0:T(8,128)}) custom-call(s32[128]{0:T(128)} %pulsar_ref.1, s32[16,1,128]{2,1,0:T(1,128)} %get-tuple-element.10.places_ref, f32[128,256]{1,0:T(8,128)} %get-tuple-element.11.weight_ref, f32[128,256]{1,0:T(8,128)} %residual_ref.3, bf16[50,128,256]{2,1,0:T(8,128)(2,1)} %bitcast.7, ...), custom_call_target="tpu_custom_call" | custom-call | tf_op jit(solution)/shard_map/local_terms/pallas_call | solution.py:324
  22.7 11.1 %gather_parts.1.sum_ref = f32[1,56,112]{2,1,0:T(8,128)} custom-call(bf16[16,56,112]{2,1,0:T(8,128)(2,1)} %get-tuple-element.13.part_ref), custom_call_target="tpu_custom_call" | custom-call | tf_op jit(solution)/shard_map/gather_parts/pallas_call | solution.py:346
  33.7 1.6 %finish.1 = (f32[50,1,100]{2,1,0:T(1,128)}, f32[1,50]{1,0:T(1,128)}) custom-call(f32[1,56,112]{2,1,0:T(8,128)} %gather_parts.1.sum_ref), custom_call_target="tpu_custom_call" | custom-call | tf_op jit(solution)/shard_map/finish/pallas_call | solution.py:359
Async XLA Ops:
  0.6 12.6 %collective-permute-start = (bf16[50,128,256]{2,1,0:T(8,128)(2,1)}, bf16[50,128,256]{2,1,0:T(8,128)(2,1)}, u32[]{:S(2)}, u32[]{:S(2)}) collective-permute-start(bf16[50,128,256]{2,1,0:T(8,128)(2,1)} %bitcast.6), channel_id=1, source_target_pairs={{0,1},{1,0},{2,3},{3,2},{4,5},{5,4},{6,7},{7,6},{8,9},{9,8},{10,11... | collective-permute-start | bytes 9830408 | tf_op jit(solution)/shard_map/ppermute | solution.py:286

commit v3 on v2

v3 whole, which is shorter than its diff:
```python
import functools

import jax
import jax.numpy as jnp
from jax import lax
from jax.experimental import pallas as pl
from jax.experimental.pallas import tpu as pltpu
from jax.sharding import PartitionSpec as P

MESH = pl.DeviceIdType.MESH
GROUP = 16
LANES = 128
VMEM_ALL = 67043328
HIGH = lax.Precision.HIGHEST


def round_up(value, step):
    return (value + step - 1) // step * step


def contract(left, right, dims, precision=None):
    return lax.dot_general(
        left, right, (dims, ((), ())), precision=precision, preferred_element_type=jnp.float32
    )


def whole_kernel(
    peers,
    pulsar_ref,
    backend_ref,
    counts_ref,
    slot_ref,
    efac_ref,
    equad_ref,
    residual_ref,
    error_ref,
    basis_ref,
    sum_ref,
    got_rows,
    got_places,
    sorted_rows,
    sorted_places,
    own_store,
    other_store,
    weights,
    lefts,
    owns,
    grams,
    part_wide,
    part,
    got_part,
    load_sems,
    swap_sends,
    swap_arrivals,
    sends,
    arrivals,
    local_sem,
):
    me = lax.axis_index("toa")
    partner = 1 - lax.axis_index("rep")
    half, tile_total, row_total = basis_ref.shape
    padded = lefts.shape[1]
    pulsar_total = efac_ref.shape[0]
    owned = pulsar_total // peers
    per_peer = tile_total // peers
    group = min(GROUP, tile_total)
    steps = tile_total // group

    barrier = pltpu.get_barrier_semaphore()
    pl.semaphore_signal(barrier, inc=1, device_id={"rep": partner}, device_id_type=MESH)

    def greet(d, carry):
        pl.semaphore_signal(
            barrier, inc=1, device_id={"toa": lax.rem(me + d, peers)}, device_id_type=MESH
        )
        return carry

    lax.fori_loop(1, peers, greet, 0)

    def chunk(ref, g):
        return ref.at[:, pl.ds(pl.multiple_of(g * group, group), group), :]

    def load(g):
        return pltpu.make_async_copy(chunk(basis_ref, g), chunk(own_store, g), load_sems.at[g])

    def swap(g):
        return pltpu.make_async_remote_copy(
            src_ref=chunk(basis_ref, g),
            dst_ref=chunk(other_store, g),
            send_sem=swap_sends.at[g],
            recv_sem=swap_arrivals.at[g],
            device_id={"rep": partner},
            device_id_type=MESH,
        )

    def each(first, last, action):
        def body(i, carry):
            action(i)
            return carry

        lax.fori_loop(first, last, body, 0)

    each(0, steps, lambda g: load(g).start())

    def onehot(row, amount):
        index = lax.broadcasted_iota(jnp.int32, (amount, tile_total), 0)
        return (index == row).astype(jnp.float32)

    pulsar_hot = onehot(pulsar_ref[...], pulsar_total)
    backend_hot = onehot(backend_ref[...], efac_ref.shape[1])

    def lookup(ref):
        columns = contract(ref[...], pulsar_hot, ((0,), (0,)), HIGH)
        return jnp.sum(columns * backend_hot, axis=0, keepdims=True)

    factor = lookup(efac_ref)
    floor_term = lookup(equad_ref)
    slot = slot_ref[...]
    dest = slot // tile_total
    place = (slot - dest * tile_total).astype(jnp.float32)
    dest_hot = onehot(dest, peers)
    earlier = (
        lax.broadcasted_iota(jnp.int32, (tile_total, tile_total), 0)
        < lax.broadcasted_iota(jnp.int32, (tile_total, tile_total), 1)
    ).astype(jnp.float32)
    before = contract(dest_hot, earlier, ((1,), (0,)))
    rank = jnp.sum(before * dest_hot, axis=0, keepdims=True)
    position = dest * per_peer + rank.astype(jnp.int32)
    order = onehot(position, tile_total)
    stacked = jnp.concatenate(
        [
            factor * factor,
            floor_term * floor_term,
            counts_ref[...].astype(jnp.float32),
            jnp.zeros((tile_total - 3, tile_total), jnp.float32),
        ],
        axis=0,
    )
    columns = jnp.transpose(stacked)
    lane = lax.broadcasted_iota(jnp.int32, (tile_total, row_total), 1).astype(jnp.float32)
    error = error_ref[...]
    weight = jnp.where(
        lane < columns[:, 2:3], 1.0 / (columns[:, 0:1] * (error * error) + columns[:, 1:2]), 0.0
    )
    weights[...] = weight
    white = jnp.sqrt(weight) * residual_ref[...]
    sorted_rows[...] = contract(order, white, ((1,), (0,)), HIGH).reshape(sorted_rows.shape)
    sorted_places[...] = contract(place, order, ((1,), (1,)), HIGH).astype(jnp.int32)
    own_rows = pltpu.make_async_copy(sorted_rows.at[me], got_rows.at[0], local_sem.at[0])
    own_places = pltpu.make_async_copy(sorted_places, got_places.at[0], local_sem.at[1])
    own_rows.start()
    own_places.start()
    pl.semaphore_wait(barrier, peers)

    def remote(source, target, n, d):
        return pltpu.make_async_remote_copy(
            src_ref=source,
            dst_ref=target,
            send_sem=sends.at[n, d],
            recv_sem=arrivals.at[n, d],
            device_id={"toa": lax.rem(me + d, peers)},
            device_id_type=MESH,
        )

    def rows_to(d):
        return remote(sorted_rows.at[lax.rem(me + d, peers)], got_rows.at[d], 0, d)

    def places_to(d):
        return remote(sorted_places, got_places.at[d], 1, d)

    def part_to(d):
        first = lax.rem(me + d, peers) * owned
        return remote(part.at[pl.ds(first, owned)], got_part.at[d], 2, d)

    each(0, steps, lambda g: swap(g).start())

    def send_rows(d):
        rows_to(d).start()
        places_to(d).start()

    each(1, peers, send_rows)

    def tiles_first(ref, g):
        block = chunk(ref, g)[...].astype(jnp.float32)
        block = jnp.concatenate(
            [block, jnp.zeros((padded - half, group, row_total), jnp.float32)], axis=0
        )
        return jnp.swapaxes(block, 0, 1)

    below = lax.broadcasted_iota(jnp.int32, (padded, row_total), 0)

    def prepare(g):
        load(g).wait()
        own = tiles_first(own_store, g)
        start = pl.multiple_of(g * group, group)
        weight = weights[pl.ds(start, group), :]
        residual = residual_ref[pl.ds(start, group), :]
        for i in range(group):
            basis = own[i]
            left = weight[i : i + 1, :] * jnp.where(below == half, residual[i : i + 1, :], basis)
            lefts[start + i] = left.astype(jnp.bfloat16)
            owns[start + i] = basis.astype(jnp.bfloat16)

    each(0, steps, prepare)

    def multiply(g):
        swap(g).wait()
        other = tiles_first(other_store, g).astype(jnp.bfloat16)
        start = pl.multiple_of(g * group, group)
        for i in range(group):
            right = jnp.concatenate([owns[start + i], other[i]], axis=0)
            grams[start + i] = contract(lefts[start + i], right, ((1,), (1,)))

    each(0, steps, multiply)

    chosen = pulsar_hot.astype(jnp.bfloat16)
    for j in range(half + 1):
        terms = grams[:, j, :]
        high = terms.astype(jnp.bfloat16)
        low = (terms - high.astype(jnp.float32)).astype(jnp.bfloat16)
        summed = contract(chosen, high, ((1,), (0,))) + contract(chosen, low, ((1,), (0,)))
        if j == half:
            coarse = summed.astype(jnp.bfloat16).astype(jnp.float32)
            part_wide[:, j, :] = coarse
            part_wide[:, j + 1, :] = summed - coarse
        else:
            part_wide[:, j, :] = summed
    for j in range(half + 2, padded):
        part_wide[:, j, :] = jnp.zeros((pulsar_total, part_wide.shape[2]), jnp.float32)
    part[...] = part_wide[...].astype(jnp.bfloat16)
    each(1, peers, lambda d: part_to(d).start())
    own_rows.wait()
    own_places.wait()

    def take_rows(d):
        rows_to(d).wait()
        places_to(d).wait()

    each(1, peers, take_rows)

    def take(d, acc):
        part_to(d).wait()
        return acc + got_part[d].astype(jnp.float32)

    mine = part[pl.ds(me * owned, owned)].astype(jnp.float32)
    sum_ref[...] = lax.fori_loop(1, peers, take, mine)


def finish_kernel(
    peers,
    half,
    places_ref,
    sum_ref,
    rows_ref,
    gram_ref,
    projection_ref,
    white_ref,
    staged,
):
    first_core = lax.axis_index("rep") == 0
    me = lax.axis_index("toa")
    padded = sum_ref.shape[1]
    per_peer, row_total = rows_ref.shape[1:]
    chunks = row_total // LANES

    def settle(d, carry):
        for i in range(per_peer):
            place = places_ref[d, 0, me * per_peer + i]
            for c in range(chunks):
                staged[c, pl.ds(place, 1), :] = rows_ref[d, i : i + 1, c * LANES : (c + 1) * LANES]
        return carry

    lax.fori_loop(0, peers, settle, 0)
    for c in range(chunks):
        white_ref[:, c * LANES : (c + 1) * LANES] = staged[c]
    for q in range(sum_ref.shape[0]):
        block = sum_ref[q]
        projection_ref[q : q + 1, :] = (
            block[half : half + 1, :half] + block[half + 1 : half + 2, :half]
        )
        mine = block[:half, :half]
        theirs = block[:half, padded : padded + half]
        gram_ref[:, q, :half] = jnp.where(first_core, mine, theirs)
        gram_ref[:, q, half:] = jnp.where(first_core, theirs, mine)


def shards(
    residual, toa_error, basis_rows, efac_table, equad_table, pulsar, backend, counts, owner_slot
):
    tile_total, row_total = residual.shape
    peers = lax.axis_size("toa")
    half = basis_rows.shape[1]
    pulsar_total = efac_table.shape[0]
    owned = pulsar_total // peers
    per_peer = tile_total // peers
    padded = round_up(half + 2, 8)
    width = 2 * padded
    steps = tile_total // min(GROUP, tile_total)
    f32 = jnp.float32
    bf16 = jnp.bfloat16
    smem = pl.BlockSpec(memory_space=pltpu.SMEM)
    vmem = pl.BlockSpec(memory_space=pltpu.VMEM)

    def row(vector):
        return vector.reshape(1, tile_total)

    summed, rows, places = pl.pallas_call(
        functools.partial(whole_kernel, peers),
        in_specs=[vmem] * 8 + [pl.BlockSpec(memory_space=pl.ANY)],
        out_specs=[vmem] * 3,
        out_shape=[
            jax.ShapeDtypeStruct((owned, padded, width), f32),
            jax.ShapeDtypeStruct((peers, per_peer, row_total), f32),
            jax.ShapeDtypeStruct((peers, 1, tile_total), jnp.int32),
        ],
        scratch_shapes=[
            pltpu.VMEM((peers, per_peer, row_total), f32),
            pltpu.VMEM((1, tile_total), jnp.int32),
            pltpu.VMEM((half, tile_total, row_total), bf16),
            pltpu.VMEM((half, tile_total, row_total), bf16),
            pltpu.VMEM((tile_total, row_total), f32),
            pltpu.VMEM((tile_total, padded, row_total), bf16),
            pltpu.VMEM((tile_total, padded, row_total), bf16),
            pltpu.VMEM((tile_total, padded, width), f32),
            pltpu.VMEM((pulsar_total, padded, width), f32),
            pltpu.VMEM((pulsar_total, padded, width), bf16),
            pltpu.VMEM((peers, owned, padded, width), bf16),
            pltpu.SemaphoreType.DMA((steps,)),
            pltpu.SemaphoreType.DMA((steps,)),
            pltpu.SemaphoreType.DMA((steps,)),
            pltpu.SemaphoreType.DMA((3, peers)),
            pltpu.SemaphoreType.DMA((3, peers)),
            pltpu.SemaphoreType.DMA((2,)),
        ],
        compiler_params=pltpu.CompilerParams(
            collective_id=0, has_side_effects=True, vmem_limit_bytes=VMEM_ALL
        ),
        name="whole",
    )(
        row(pulsar),
        row(backend),
        row(counts),
        row(owner_slot),
        efac_table,
        equad_table,
        residual,
        toa_error,
        jnp.transpose(basis_rows, (1, 0, 2)),
    )
    gram, projection, whitened = pl.pallas_call(
        functools.partial(finish_kernel, peers, half),
        in_specs=[smem, vmem, vmem],
        out_specs=[vmem] * 3,
        out_shape=[
            jax.ShapeDtypeStruct((half, owned, 2 * half), f32),
            jax.ShapeDtypeStruct((owned, half), f32),
            jax.ShapeDtypeStruct((tile_total, row_total), f32),
        ],
        scratch_shapes=[pltpu.VMEM((row_total // LANES, tile_total, LANES), f32)],
        name="finish",
    )(places, summed, rows)
    return (jnp.transpose(gram, (1, 2, 0)), projection, whitened)


def solution(mesh):
    in_specs = (
        P("toa", None),
        P("toa", None),
        P("toa", "rep", None),
        P(),
        P(),
        P("toa"),
        P("toa"),
        P("toa"),
        P("toa"),
    )
    out_specs = (P("toa", None, "rep"), P("toa", "rep"), P("toa", None))
    return jax.shard_map(shards, mesh=mesh, in_specs=in_specs, out_specs=out_specs, check_vma=False)
```

time: 35.7 us -> 32.4 us (0.908)
  Pallas kernels: 34.1 us -> 31.5 us
  starting transfers between devices: 0.56 us -> 0 us
    pallas_call x4 -> x2, Pallas kernels: 34.1 us -> 31.5 us  [the longest x1 29.4 us: shards(): pl.pallas_call(functools.partial(whole_kernel, peers), in_specs=[vmem] *...]
    ppermute x1 -> x0, starting transfers between devices: 0.56 us -> none  [shards(): other = lax.ppermute(own, 'rep', [(0, 1), (1, 0)])]
  transfers between devices with their start and end apart: 1 -> 0, of which waited for: 0 -> 0; matrix products, arithmetic and copies ran while one was open for 0% -> 0% of each run, Pallas kernels for 34% -> 0%
where the time goes in v3:
time: 32.4 us; the launch traced here: 32.2 us
  Pallas kernels  31.5 us (97%)
  between operations  0.64 us (2%)
    pallas_call x1, Pallas kernels, shards(): pl.pallas_call(functools.partial(whole_kernel, peers), in_specs=[vmem] *...  29.4 us
    pallas_call x1, Pallas kernels, shards(): pl.pallas_call(functools.partial(finish_kernel, peers, half), in_specs=[s...  2.1 us

profile of v3, /device:TPU:0, one launch (start us, length us, event | category | flops | bytes accessed | tf_op | source)
XLA Modules:
  0.0 32.2 jit_solution(8948342076782038680)
XLA Ops:
  0.6 29.4 %whole.1 = (f32[1,56,112]{2,1,0:T(8,128)}, f32[16,8,256]{2,1,0:T(8,128)}, s32[16,1,128]{2,1,0:T(1,128)}) custom-call(s32[1,128]{1,0:T(1,128)} %bitcast.7, s32[1,128]{1,0:T(1,128)} %bitcast.8, s32[1,128]{1,0:T(1,128)} %bitcast.9, s32[1,128]{1,0:T(1,128)} %bitcast.10, f32[16,64]{1,0:T(8,128)} %efac_ref.1, f32[16,64]{1,0:T(8,128)} %equad_ref.1, ...), custom_call_target="tpu_custom_call" | custom-call | tf_op jit(solution)/shard_map/whole/pallas_call | solution.py:307
  30.1 2.1 %finish.1 = (f32[50,1,100]{2,1,0:T(1,128)}, f32[1,50]{1,0:T(1,128)}, f32[128,256]{1,0:T(8,128)}) custom-call(s32[16,1,128]{2,1,0:T(1,128)} %get-tuple-element.9.places_ref, f32[1,56,112]{2,1,0:T(8,128)} %get-tuple-element.10.sum_ref, f32[16,8,256]{2,1,0:T(8,128)} %get-tuple-element.11.rows_ref), custom_call_target="tpu_custom_call" | custom-call | tf_op jit(solution)/shard_map/finish/pallas_call | solution.py:350

commit v4 on v3

--- a/solution.py
+++ b/solution.py
@@ -203,31 +203,39 @@
 
     each(0, steps, prepare)
 
+    blank = jnp.zeros((grams.shape[1] - 2 * padded, row_total), jnp.bfloat16)
+
     def multiply(g):
         swap(g).wait()
         other = tiles_first(other_store, g).astype(jnp.bfloat16)
         start = pl.multiple_of(g * group, group)
         for i in range(group):
-            right = jnp.concatenate([owns[start + i], other[i]], axis=0)
-            grams[start + i] = contract(lefts[start + i], right, ((1,), (1,)))
+            right = jnp.concatenate([owns[start + i], other[i], blank], axis=0)
+            row = pl.multiple_of((start + i) * padded, 8)
+            grams[pl.ds(row, padded), :] = contract(lefts[start + i], right, ((1,), (1,)))
 
     each(0, steps, multiply)
 
     chosen = pulsar_hot.astype(jnp.bfloat16)
-    for j in range(half + 1):
-        terms = grams[:, j, :]
+    chosen = jnp.concatenate([chosen, chosen], axis=1)
+    for j in range(padded):
+        into = pl.ds(j, pulsar_total, stride=padded)
+        if j > half + 1:
+            part_wide[into, :] = jnp.zeros((pulsar_total, part_wide.shape[1]), jnp.float32)
+            continue
+        if j == half + 1:
+            continue
+        terms = grams[pl.ds(j, tile_total, stride=padded), :]
         high = terms.astype(jnp.bfloat16)
         low = (terms - high.astype(jnp.float32)).astype(jnp.bfloat16)
-        summed = contract(chosen, high, ((1,), (0,))) + contract(chosen, low, ((1,), (0,)))
+        summed = contract(chosen, jnp.concatenate([high, low], axis=0), ((1,), (0,)))
         if j == half:
             coarse = summed.astype(jnp.bfloat16).astype(jnp.float32)
-            part_wide[:, j, :] = coarse
-            part_wide[:, j + 1, :] = summed - coarse
+            part_wide[into, :] = coarse
+            part_wide[pl.ds(j + 1, pulsar_total, stride=padded), :] = summed - coarse
         else:
-            part_wide[:, j, :] = summed
-    for j in range(half + 2, padded):
-        part_wide[:, j, :] = jnp.zeros((pulsar_total, part_wide.shape[2]), jnp.float32)
-    part[...] = part_wide[...].astype(jnp.bfloat16)
+            part_wide[into, :] = summed
+    part[...] = part_wide[...].reshape(part.shape).astype(jnp.bfloat16)
     each(1, peers, lambda d: part_to(d).start())
     own_rows.wait()
     own_places.wait()
@@ -294,7 +302,7 @@
     owned = pulsar_total // peers
     per_peer = tile_total // peers
     padded = round_up(half + 2, 8)
-    width = 2 * padded
+    width = round_up(2 * padded, LANES)
     steps = tile_total // min(GROUP, tile_total)
     f32 = jnp.float32
     bf16 = jnp.bfloat16
@@ -321,8 +329,8 @@
             pltpu.VMEM((tile_total, row_total), f32),
             pltpu.VMEM((tile_total, padded, row_total), bf16),
             pltpu.VMEM((tile_total, padded, row_total), bf16),
-            pltpu.VMEM((tile_total, padded, width), f32),
-            pltpu.VMEM((pulsar_total, padded, width), f32),
+            pltpu.VMEM((tile_total * padded, width), f32),
+            pltpu.VMEM((pulsar_total * padded, width), f32),
             pltpu.VMEM((pulsar_total, padded, width), bf16),
             pltpu.VMEM((peers, owned, padded, width), bf16),
             pltpu.SemaphoreType.DMA((steps,)),

time: 32.4 us -> 24.4 us (0.75)
  Pallas kernels: 31.5 us -> 23.5 us
    pallas_call x1, Pallas kernels: 29.4 us -> 21.4 us  [shards(): pl.pallas_call(functools.partial(whole_kernel, peers), in_specs=[vmem] *...]
where the time goes in v4:
time: 24.4 us; the launch traced here: 24.2 us
  Pallas kernels  23.5 us (96%)
  between operations  0.64 us (3%)
    pallas_call x1, Pallas kernels, shards(): pl.pallas_call(functools.partial(whole_kernel, peers), in_specs=[vmem] *...  21.4 us
    pallas_call x1, Pallas kernels, shards(): pl.pallas_call(functools.partial(finish_kernel, peers, half), in_specs=[s...  2.1 us

profile of v4, /device:TPU:0, one launch (start us, length us, event | category | flops | bytes accessed | tf_op | source)
XLA Modules:
  0.0 24.2 jit_solution(13854484055061780126)
XLA Ops:
  0.6 21.4 %whole.1 = (f32[1,56,128]{2,1,0:T(8,128)}, f32[16,8,256]{2,1,0:T(8,128)}, s32[16,1,128]{2,1,0:T(1,128)}) custom-call(s32[1,128]{1,0:T(1,128)} %bitcast.7, s32[1,128]{1,0:T(1,128)} %bitcast.8, s32[1,128]{1,0:T(1,128)} %bitcast.9, s32[1,128]{1,0:T(1,128)} %bitcast.10, f32[16,64]{1,0:T(8,128)} %efac_ref.1, f32[16,64]{1,0:T(8,128)} %equad_ref.1, ...), custom_call_target="tpu_custom_call" | custom-call | tf_op jit(solution)/shard_map/whole/pallas_call | solution.py:315
  22.1 2.1 %finish.1 = (f32[50,1,100]{2,1,0:T(1,128)}, f32[1,50]{1,0:T(1,128)}, f32[128,256]{1,0:T(8,128)}) custom-call(s32[16,1,128]{2,1,0:T(1,128)} %get-tuple-element.9.places_ref, f32[1,56,128]{2,1,0:T(8,128)} %get-tuple-element.10.sum_ref, f32[16,8,256]{2,1,0:T(8,128)} %get-tuple-element.11.rows_ref), custom_call_target="tpu_custom_call" | custom-call | tf_op jit(solution)/shard_map/finish/pallas_call | solution.py:358

commit v5 on v4

--- a/solution.py
+++ b/solution.py
@@ -36,6 +36,7 @@
     error_ref,
     basis_ref,
     sum_ref,
+    partner_sum,
     got_rows,
     got_places,
     sorted_rows,
@@ -55,9 +56,11 @@
     sends,
     arrivals,
     local_sem,
+    last_sems,
 ):
     me = lax.axis_index("toa")
-    partner = 1 - lax.axis_index("rep")
+    core = lax.axis_index("rep")
+    partner = 1 - core
     half, tile_total, row_total = basis_ref.shape
     padded = lefts.shape[1]
     pulsar_total = efac_ref.shape[0]
@@ -65,6 +68,7 @@
     per_peer = tile_total // peers
     group = min(GROUP, tile_total)
     steps = tile_total // group
+    swaps = steps // 2
 
     barrier = pltpu.get_barrier_semaphore()
     pl.semaphore_signal(barrier, inc=1, device_id={"rep": partner}, device_id_type=MESH)
@@ -85,7 +89,7 @@
 
     def swap(g):
         return pltpu.make_async_remote_copy(
-            src_ref=chunk(basis_ref, g),
+            src_ref=chunk(basis_ref, partner * swaps + g),
             dst_ref=chunk(other_store, g),
             send_sem=swap_sends.at[g],
             recv_sem=swap_arrivals.at[g],
@@ -172,7 +176,7 @@
         first = lax.rem(me + d, peers) * owned
         return remote(part.at[pl.ds(first, owned)], got_part.at[d], 2, d)
 
-    each(0, steps, lambda g: swap(g).start())
+    each(0, swaps, lambda g: swap(g).start())
 
     def send_rows(d):
         rows_to(d).start()
@@ -204,17 +208,25 @@
     each(0, steps, prepare)
 
     blank = jnp.zeros((grams.shape[1] - 2 * padded, row_total), jnp.bfloat16)
-
-    def multiply(g):
+    absent = jnp.zeros((grams.shape[1] - padded, row_total), jnp.bfloat16)
+
+    def multiply(tile, rest):
+        right = jnp.concatenate([owns[tile]] + rest, axis=0)
+        row = pl.multiple_of(tile * padded, 8)
+        grams[pl.ds(row, padded), :] = contract(lefts[tile], right, ((1,), (1,)))
+
+    def alone(g):
+        for i in range(group):
+            multiply((partner * swaps + g) * group + i, [absent])
+
+    def crossed(g):
         swap(g).wait()
         other = tiles_first(other_store, g).astype(jnp.bfloat16)
-        start = pl.multiple_of(g * group, group)
         for i in range(group):
-            right = jnp.concatenate([owns[start + i], other[i], blank], axis=0)
-            row = pl.multiple_of((start + i) * padded, 8)
-            grams[pl.ds(row, padded), :] = contract(lefts[start + i], right, ((1,), (1,)))
-
-    each(0, steps, multiply)
+            multiply((core * swaps + g) * group + i, [other[i], blank])
+
+    each(0, swaps, alone)
+    each(0, swaps, crossed)
 
     chosen = pulsar_hot.astype(jnp.bfloat16)
     chosen = jnp.concatenate([chosen, chosen], axis=1)
@@ -252,6 +264,16 @@
 
     mine = part[pl.ds(me * owned, owned)].astype(jnp.float32)
     sum_ref[...] = lax.fori_loop(1, peers, take, mine)
+    last = pltpu.make_async_remote_copy(
+        src_ref=sum_ref,
+        dst_ref=partner_sum,
+        send_sem=last_sems.at[0],
+        recv_sem=last_sems.at[1],
+        device_id={"rep": partner},
+        device_id_type=MESH,
+    )
+    last.start()
+    last.wait()
 
 
 def finish_kernel(
@@ -259,6 +281,7 @@
     half,
     places_ref,
     sum_ref,
+    partner_ref,
     rows_ref,
     gram_ref,
     projection_ref,
@@ -287,7 +310,8 @@
             block[half : half + 1, :half] + block[half + 1 : half + 2, :half]
         )
         mine = block[:half, :half]
-        theirs = block[:half, padded : padded + half]
+        turned = jnp.transpose(partner_ref[q][:, padded : 2 * padded])
+        theirs = block[:half, padded : padded + half] + turned[:half, :half]
         gram_ref[:, q, :half] = jnp.where(first_core, mine, theirs)
         gram_ref[:, q, half:] = jnp.where(first_core, theirs, mine)
 
@@ -312,11 +336,12 @@
     def row(vector):
         return vector.reshape(1, tile_total)
 
-    summed, rows, places = pl.pallas_call(
+    summed, partner_summed, rows, places = pl.pallas_call(
         functools.partial(whole_kernel, peers),
         in_specs=[vmem] * 8 + [pl.BlockSpec(memory_space=pl.ANY)],
-        out_specs=[vmem] * 3,
+        out_specs=[vmem] * 4,
         out_shape=[
+            jax.ShapeDtypeStruct((owned, padded, width), f32),
             jax.ShapeDtypeStruct((owned, padded, width), f32),
             jax.ShapeDtypeStruct((peers, per_peer, row_total), f32),
             jax.ShapeDtypeStruct((peers, 1, tile_total), jnp.int32),
@@ -325,7 +350,7 @@
             pltpu.VMEM((peers, per_peer, row_total), f32),
             pltpu.VMEM((1, tile_total), jnp.int32),
             pltpu.VMEM((half, tile_total, row_total), bf16),
-            pltpu.VMEM((half, tile_total, row_total), bf16),
+            pltpu.VMEM((half, tile_total // 2, row_total), bf16),
             pltpu.VMEM((tile_total, row_total), f32),
             pltpu.VMEM((tile_total, padded, row_total), bf16),
             pltpu.VMEM((tile_total, padded, row_total), bf16),
@@ -334,10 +359,11 @@
             pltpu.VMEM((pulsar_total, padded, width), bf16),
             pltpu.VMEM((peers, owned, padded, width), bf16),
             pltpu.SemaphoreType.DMA((steps,)),
-            pltpu.SemaphoreType.DMA((steps,)),
-            pltpu.SemaphoreType.DMA((steps,)),
+            pltpu.SemaphoreType.DMA((steps // 2,)),
+            pltpu.SemaphoreType.DMA((steps // 2,)),
             pltpu.SemaphoreType.DMA((3, peers)),
             pltpu.SemaphoreType.DMA((3, peers)),
+            pltpu.SemaphoreType.DMA((2,)),
             pltpu.SemaphoreType.DMA((2,)),
         ],
         compiler_params=pltpu.CompilerParams(
@@ -357,7 +383,7 @@
     )
     gram, projection, whitened = pl.pallas_call(
         functools.partial(finish_kernel, peers, half),
-        in_specs=[smem, vmem, vmem],
+        in_specs=[smem, vmem, vmem, vmem],
         out_specs=[vmem] * 3,
         out_shape=[
             jax.ShapeDtypeStruct((half, owned, 2 * half), f32),
@@ -366,7 +392,7 @@
         ],
         scratch_shapes=[pltpu.VMEM((row_total // LANES, tile_total, LANES), f32)],
         name="finish",
-    )(places, summed, rows)
+    )(places, summed, partner_summed, rows)
     return (jnp.transpose(gram, (1, 2, 0)), projection, whitened)
 
 

time: 24.4 us -> 23.8 us (0.975)
  Pallas kernels: 23.5 us -> 23 us
    pallas_call x1, Pallas kernels: 21.4 us -> 20.7 us  [shards(): pl.pallas_call(functools.partial(whole_kernel, peers), in_specs=[vmem] *...]
where the time goes in v5:
time: 23.8 us; the launch traced here: 23.6 us
  Pallas kernels  23 us (97%)
  between operations  0.64 us (3%)
    pallas_call x1, Pallas kernels, shards(): pl.pallas_call(functools.partial(whole_kernel, peers), in_specs=[vmem] *...  20.7 us
    pallas_call x1, Pallas kernels, shards(): pl.pallas_call(functools.partial(finish_kernel, peers, half), in_specs=[s...  2.27 us

profile of v5, /device:TPU:0, one launch (start us, length us, event | category | flops | bytes accessed | tf_op | source)
XLA Modules:
  0.0 23.6 jit_solution(12788304447118030081)
XLA Ops:
  0.6 20.7 %whole.1 = (f32[1,56,128]{2,1,0:T(8,128)}, f32[1,56,128]{2,1,0:T(8,128)}, f32[16,8,256]{2,1,0:T(8,128)}, s32[16,1,128]{2,1,0:T(1,128)}) custom-call(s32[1,128]{1,0:T(1,128)} %bitcast.7, s32[1,128]{1,0:T(1,128)} %bitcast.8, s32[1,128]{1,0:T(1,128)} %bitcast.9, s32[1,128]{1,0:T(1,128)} %bitcast.10, f32[16,64]{1,0:T(8,128)} %efac_ref.1, f32[16,64]{1,0:T(8,128)} %equad_ref.1, ...), custom_call_target="tpu_custom_call" | custom-call | tf_op jit(solution)/shard_map/whole/pallas_call | solution.py:339
  21.3 2.3 %finish.1 = (f32[50,1,100]{2,1,0:T(1,128)}, f32[1,50]{1,0:T(1,128)}, f32[128,256]{1,0:T(8,128)}) custom-call(s32[16,1,128]{2,1,0:T(1,128)} %get-tuple-element.10.places_ref, f32[1,56,128]{2,1,0:T(8,128)} %get-tuple-element.11.sum_ref, f32[1,56,128]{2,1,0:T(8,128)} %get-tuple-element.12.partner_ref, f32[16,8,256]{2,1,0:T(8,128)} %get-tuple-element.13.rows_ref), custom_call_target="tpu_custom_call" | custom-call | tf_op jit(solution)/shard_map/finish/pallas_call | solution.py:384

commit v6 on v5

--- a/solution.py
+++ b/solution.py
@@ -154,35 +154,6 @@
     own_places = pltpu.make_async_copy(sorted_places, got_places.at[0], local_sem.at[1])
     own_rows.start()
     own_places.start()
-    pl.semaphore_wait(barrier, peers)
-
-    def remote(source, target, n, d):
-        return pltpu.make_async_remote_copy(
-            src_ref=source,
-            dst_ref=target,
-            send_sem=sends.at[n, d],
-            recv_sem=arrivals.at[n, d],
-            device_id={"toa": lax.rem(me + d, peers)},
-            device_id_type=MESH,
-        )
-
-    def rows_to(d):
-        return remote(sorted_rows.at[lax.rem(me + d, peers)], got_rows.at[d], 0, d)
-
-    def places_to(d):
-        return remote(sorted_places, got_places.at[d], 1, d)
-
-    def part_to(d):
-        first = lax.rem(me + d, peers) * owned
-        return remote(part.at[pl.ds(first, owned)], got_part.at[d], 2, d)
-
-    each(0, swaps, lambda g: swap(g).start())
-
-    def send_rows(d):
-        rows_to(d).start()
-        places_to(d).start()
-
-    each(1, peers, send_rows)
 
     def tiles_first(ref, g):
         block = chunk(ref, g)[...].astype(jnp.float32)
@@ -206,6 +177,35 @@
             owns[start + i] = basis.astype(jnp.bfloat16)
 
     each(0, steps, prepare)
+    pl.semaphore_wait(barrier, peers)
+
+    def remote(source, target, n, d):
+        return pltpu.make_async_remote_copy(
+            src_ref=source,
+            dst_ref=target,
+            send_sem=sends.at[n, d],
+            recv_sem=arrivals.at[n, d],
+            device_id={"toa": lax.rem(me + d, peers)},
+            device_id_type=MESH,
+        )
+
+    def rows_to(d):
+        return remote(sorted_rows.at[lax.rem(me + d, peers)], got_rows.at[d], 0, d)
+
+    def places_to(d):
+        return remote(sorted_places, got_places.at[d], 1, d)
+
+    def part_to(d):
+        first = lax.rem(me + d, peers) * owned
+        return remote(part.at[pl.ds(first, owned)], got_part.at[d], 2, d)
+
+    each(0, swaps, lambda g: swap(g).start())
+
+    def send_rows(d):
+        rows_to(d).start()
+        places_to(d).start()
+
+    each(1, peers, send_rows)
 
     blank = jnp.zeros((grams.shape[1] - 2 * padded, row_total), jnp.bfloat16)
     absent = jnp.zeros((grams.shape[1] - padded, row_total), jnp.bfloat16)

time: 23.8 us -> 23.8 us (level)
  the two profiles are of different devices: /device:TPU:0 before, /device:TPU:9 now
where the time goes in v6:
time: 23.8 us; the launch traced here: 23.7 us
  Pallas kernels  23 us (97%)
  between operations  0.64 us (3%)
    pallas_call x1, Pallas kernels, shards(): pl.pallas_call(functools.partial(whole_kernel, peers), in_specs=[vmem] *...  20.8 us
    pallas_call x1, Pallas kernels, shards(): pl.pallas_call(functools.partial(finish_kernel, peers, half), in_specs=[s...  2.27 us

profile of v6, /device:TPU:9, one launch (start us, length us, event | category | flops | bytes accessed | tf_op | source)
XLA Modules:
  0.0 23.7 jit_solution(14617591943516105738)
XLA Ops:
  0.6 20.8 %whole.1 = (f32[1,56,128]{2,1,0:T(8,128)}, f32[1,56,128]{2,1,0:T(8,128)}, f32[16,8,256]{2,1,0:T(8,128)}, s32[16,1,128]{2,1,0:T(1,128)}) custom-call(s32[1,128]{1,0:T(1,128)} %bitcast.7, s32[1,128]{1,0:T(1,128)} %bitcast.8, s32[1,128]{1,0:T(1,128)} %bitcast.9, s32[1,128]{1,0:T(1,128)} %bitcast.10, f32[16,64]{1,0:T(8,128)} %efac_ref.1, f32[16,64]{1,0:T(8,128)} %equad_ref.1, ...), custom_call_target="tpu_custom_call" | custom-call | tf_op jit(solution)/shard_map/whole/pallas_call | solution.py:339
  21.4 2.3 %finish.1 = (f32[50,1,100]{2,1,0:T(1,128)}, f32[1,50]{1,0:T(1,128)}, f32[128,256]{1,0:T(8,128)}) custom-call(s32[16,1,128]{2,1,0:T(1,128)} %get-tuple-element.10.places_ref, f32[1,56,128]{2,1,0:T(8,128)} %get-tuple-element.11.sum_ref, f32[1,56,128]{2,1,0:T(8,128)} %get-tuple-element.12.partner_ref, f32[16,8,256]{2,1,0:T(8,128)} %get-tuple-element.13.rows_ref), custom_call_target="tpu_custom_call" | custom-call | tf_op jit(solution)/shard_map/finish/pallas_call | solution.py:384
